TPU v7x, 32 devices: a whole 2x2x4 slice. The times are simulated.
32 devices in a mesh: ep: 8 (over z, y), tp: 4 (over x, core).
Axes of the slice: x: 2, y: 2, z: 4, core: 2. Of those that a mesh axis runs over, the one named last changes fastest.
Arguments:
- tokens: bfloat16 [1024, 4096], P('ep', 'tp'), may hold values from -6 to 6
- out_grad: bfloat16 [1024, 4096], P('ep', 'tp'), may hold values from -6 to 6
- expert_ids: int32 [1024, 4], P('ep'), may hold values from 0 to 7, all different within a row; in each aligned block of 128 rows (0 to 127, 128 to 255, ...) at most 72 rows name the same one
- route_probs: float32 [1024, 4], P('ep'), may hold values from 0.05 to 0.5
- w_gate: bfloat16 [8, 4096, 768], P('ep', 'tp'), may hold values from -0.09375 to 0.09375
- w_up: bfloat16 [8, 4096, 768], P('ep', 'tp'), may hold values from -0.09375 to 0.09375
- w_down: bfloat16 [8, 768, 4096], P('ep', None, 'tp'), may hold values from -0.21875 to 0.21875
Outputs:
- grad_tokens: bfloat16 [1024, 4096], P('ep', 'tp')
- fisher_gate: bfloat16 [8, 4096, 768], P('ep', 'tp')
- fisher_up: bfloat16 [8, 4096, 768], P('ep', 'tp')
- fisher_down: bfloat16 [8, 768, 4096], P('ep', None, 'tp')
Inputs may be any that keep to these rules, and one draw needn't show every extreme that they name: `expert_ids`: each token names 4 different experts; among the tokens of one index of ep no expert is named by more than 72 tokens, a bound that some block reaches.
All inputs are finite; a program needn't handle non-finite values.
Results may differ from a plain program's by a relative error of at most 0.03.
Values may be sent and summed in bfloat16 or wider, within the bound.
A program may use at most 128 MiB of HBM per device.

v0:
```python
import jax
import jax.numpy as jnp
from jax import lax
from jax.sharding import PartitionSpec as P


def contract_rows(left, right):
    return lax.dot_general(
        left, right, (((0,), (0,)), ((), ())), preferred_element_type=jnp.float32
    )


def contract_cols(left, right):
    return lax.dot_general(
        left, right, (((1,), (1,)), ((), ())), preferred_element_type=jnp.float32
    )


def swiglu_back(gate, up, dact):
    sig = jax.nn.sigmoid(gate)
    act = (gate * sig * up).astype(jnp.bfloat16)
    dgate = (dact * up * sig * (1.0 + gate * (1.0 - sig))).astype(jnp.bfloat16)
    dup = (dact * gate * sig).astype(jnp.bfloat16)
    return (act, dgate, dup)


def squared(values):
    return jnp.square(values.astype(jnp.float32)).astype(jnp.bfloat16)


def on_device(tokens, out_grad, expert_ids, route_probs, w_gate, w_up, w_down):
    tok_rows = tokens.shape[0]
    width_part = tokens.shape[1]
    top_count = expert_ids.shape[1]
    experts = lax.axis_size("ep")
    capacity = tok_rows * top_count * 9 // (8 * experts)
    assigns = tok_rows * top_count
    flat_ids = expert_ids.reshape(-1)
    onehot = (flat_ids[:, None] == jnp.arange(experts, dtype=jnp.int32)[None, :]).astype(jnp.int32)
    ranks = jnp.sum((jnp.cumsum(onehot, 0) - onehot) * onehot, 1)
    slot_index = flat_ids * capacity + ranks
    table = (
        jnp.full((experts * capacity,), assigns, jnp.int32)
        .at[slot_index]
        .set(jnp.arange(assigns, dtype=jnp.int32))
    )
    token_of = table // top_count
    padded_x = jnp.concatenate([tokens, jnp.zeros((1, width_part), tokens.dtype)], 0)
    padded_dy = jnp.concatenate([out_grad, jnp.zeros((1, width_part), out_grad.dtype)], 0)
    padded_p = jnp.concatenate([route_probs.reshape(-1), jnp.zeros((1,), jnp.float32)], 0)
    send_x = padded_x[token_of].reshape(experts, capacity, width_part)
    send_dy = (padded_dy[token_of].astype(jnp.float32) * padded_p[table][:, None]).astype(
        jnp.bfloat16
    )
    send_dy = send_dy.reshape(experts, capacity, width_part)
    gate_mat = w_gate[0]
    up_mat = w_up[0]
    down_mat = w_down[0]
    recv_x, recv_dy = (
        lax.all_to_all(send_x, "ep", split_axis=0, concat_axis=0, tiled=True),
        lax.all_to_all(send_dy, "ep", split_axis=0, concat_axis=0, tiled=True),
    )
    recv_x = recv_x.reshape(-1, width_part)
    recv_dy = recv_dy.reshape(-1, width_part)
    gate_part = jnp.dot(recv_x, gate_mat, preferred_element_type=jnp.float32)
    up_part = jnp.dot(recv_x, up_mat, preferred_element_type=jnp.float32)
    dact_part = contract_cols(recv_dy, down_mat)
    gate, up, dact = (
        lax.psum(gate_part.astype(jnp.bfloat16), "tp").astype(jnp.float32),
        lax.psum(up_part.astype(jnp.bfloat16), "tp").astype(jnp.float32),
        lax.psum(dact_part.astype(jnp.bfloat16), "tp").astype(jnp.float32),
    )
    act, dgate, dup = swiglu_back(gate, up, dact)
    dx_rows = (contract_cols(dgate, gate_mat) + contract_cols(dup, up_mat)).astype(jnp.bfloat16)
    returned = lax.all_to_all(
        dx_rows.reshape(experts, capacity, width_part),
        "ep",
        split_axis=0,
        concat_axis=0,
        tiled=True,
    )
    scale = 1.0 / tok_rows
    x_sq = squared(recv_x)
    fisher_gate = (contract_rows(x_sq, squared(dgate)) * scale).astype(jnp.bfloat16)[None]
    fisher_up = (contract_rows(x_sq, squared(dup)) * scale).astype(jnp.bfloat16)[None]
    fisher_down = (contract_rows(squared(act), squared(recv_dy)) * scale).astype(jnp.bfloat16)[None]
    pulled = returned.reshape(experts * capacity, width_part)[slot_index].astype(jnp.float32)
    grad_tokens = jnp.sum(pulled.reshape(tok_rows, top_count, width_part), 1).astype(jnp.bfloat16)
    return (grad_tokens, fisher_gate, fisher_up, fisher_down)


def solution(mesh):
    in_specs = (
        P("ep", "tp"),
        P("ep", "tp"),
        P("ep", None),
        P("ep", None),
        P("ep", "tp", None),
        P("ep", "tp", None),
        P("ep", None, "tp"),
    )
    out_specs = (P("ep", "tp"), P("ep", "tp", None), P("ep", "tp", None), P("ep", None, "tp"))
    return jax.shard_map(
        on_device, mesh=mesh, in_specs=in_specs, out_specs=out_specs, check_vma=False
    )
```

profile of v0, /device:TPU:0, one launch (start us, length us, event | category | flops | bytes accessed | tf_op | source)
XLA Modules:
  0.0 202.3 jit_solution(541118483908250791)
XLA Ops:
  7.2 0.8 broadcast_multiply_fusion
  8.0 0.8 copy.12
  8.9 0.1 eq.25
  9.0 0.1 copy.11
  9.1 0.1 mul.68
  9.2 1.1 reduce-window.6
  10.4 0.2 slice_reduce_fusion
  10.7 2.4 %scatter_custom_fusion = s32[576]{0:T(1024)S(1)} fusion(s32[512]{0:T(512)S(1)} %bitcast.50, s32[512]{0:T(512)S(1)} %iota.11, s32[]{:T(128)} %constant.15.clone.1), kind=kCustom, calls=%fused_computation.68 | custom fusion | bytes 2308 | tf_op jit(solution)/shard_map/scatter | solution.py:45
  13.2 1.0 concatenate.11
  14.2 3.4 %gather_fusion.2 = bf16[576,1024]{1,0:T(8,128)(2,1)} fusion(bf16[129,1024]{1,0:T(8,128)(2,1)S(1)} %concatenate.11, s32[1024]{0:T(1024)S(1)} %get-tuple-element.10), kind=kCustom, calls=%fused_computation.2 | custom fusion | bytes 2361600 | tf_op jit(solution)/shard_map/gather | solution.py:51
  17.6 7.4 %all-to-all-start.1 = ((bf16[8,72,1024]{2,1,0:T(8,128)(2,1)}), bf16[8,72,1024]{2,1,0:T(8,128)(2,1)}, u32[]{:S(2)}, u32[]{:S(2)}) async-start(bf16[8,72,1024]{2,1,0:T(8,128)(2,1)} %bitcast.7), calls=%async_computation.1 | async-start | bytes 2359296 | tf_op jit(solution)/shard_map/all_to_all | solution.py:60
  25.1 2.9 %gather_fusion = bf16[576,1024]{1,0:T(8,128)(2,1)S(1)} fusion(bf16[129,1024]{1,0:T(8,128)(2,1)S(1)} %concatenate.9, s32[1024]{0:T(1024)S(1)} %get-tuple-element.10), kind=kCustom, calls=%fused_computation | custom fusion | bytes 2361600 | tf_op jit(solution)/shard_map/gather | solution.py:52
  28.0 0.1 copy.14
  28.2 2.6 %gather_fusion.1 = f32[576]{0:T(1024)S(1)} fusion(f32[513]{0:T(1024)S(1)} %pad_maximum_fusion, s32[1024]{0:T(1024)S(1)} %get-tuple-element.9), kind=kCustom, calls=%fused_computation.1 | custom fusion | bytes 6912 | tf_op jit(solution)/shard_map/gather | solution.py:52
  30.9 1.3 fusion
  32.2 21.6 %all-to-all-done.1 = bf16[8,72,1024]{2,1,0:T(8,128)(2,1)} async-done(((bf16[8,72,1024]{2,1,0:T(8,128)(2,1)}), bf16[8,72,1024]{2,1,0:T(8,128)(2,1)}, u32[]{:S(2)}, u32[]{:S(2)}) %all-to-all-start.1) | async-done | bytes 1179680 | tf_op jit(solution)/shard_map/all_to_all | solution.py:60
  53.8 3.6 %all-to-all-start = ((bf16[8,72,1024]{2,1,0:T(8,128)(2,1)}), bf16[8,72,1024]{2,1,0:T(8,128)(2,1)S(1)}, u32[]{:S(2)}, u32[]{:S(2)}) async-start(bf16[8,72,1024]{2,1,0:T(8,128)(2,1)} %fusion), calls=%async_computation | async-start | bytes 2359296 | tf_op jit(solution)/shard_map/all_to_all | solution.py:61
  57.4 3.8 %fusion.26 = bf16[576,768]{1,0:T(8,128)(2,1)} fusion(bf16[576,1024]{1,0:T(8,128)(2,1)} %bitcast.8, bf16[1,1024,768]{2,1,0:T(8,128)(2,1)} %param.12), kind=kOutput, calls=%fused_computation.45 | convolution fusion | flops 906412032 | bytes 3637248 | tf_op jit(solution)/shard_map/dot_general | solution.py:66
  61.2 3.3 %fusion.29 = bf16[576,768]{1,0:T(8,128)(2,1)} fusion(bf16[576,1024]{1,0:T(8,128)(2,1)} %bitcast.8, bf16[1,1024,768]{2,1,0:T(8,128)(2,1)S(1)} %copy-done), kind=kOutput, calls=%fused_computation.46 | convolution fusion | flops 906412032 | bytes 3637248 | tf_op jit(solution)/shard_map/dot_general | solution.py:65
  64.5 21.6 %all-to-all-done = bf16[8,72,1024]{2,1,0:T(8,128)(2,1)S(1)} async-done(((bf16[8,72,1024]{2,1,0:T(8,128)(2,1)}), bf16[8,72,1024]{2,1,0:T(8,128)(2,1)S(1)}, u32[]{:S(2)}, u32[]{:S(2)}) %all-to-all-start) | async-done | bytes 1179680 | tf_op jit(solution)/shard_map/all_to_all | solution.py:61
  86.1 3.9 %fusion.23 = bf16[576,768]{1,0:T(8,128)(2,1)} fusion(bf16[576,1024]{1,0:T(8,128)(2,1)S(1)} %bitcast.47, bf16[1,768,1024]{2,1,0:T(8,128)(2,1)} %param.13), kind=kOutput, calls=%fused_computation.44 | convolution fusion | flops 906412032 | bytes 3637248 | tf_op jit(solution)/shard_map/dot_general | solution.py:14
  90.0 59.7 %all-reduce.5.cloned.1.call-done = (bf16[576,768]{1,0:T(8,128)(2,1)}, bf16[576,768]{1,0:T(8,128)(2,1)}, bf16[576,768]{1,0:T(8,128)(2,1)}) async-done(((bf16[576,768]{1,0:T(8,128)(2,1)}, bf16[576,768]{1,0:T(8,128)(2,1)}, bf16[576,768]{1,0:T(8,128)(2,1)}), (bf16[576,768]{1,0:T(8,128)(2,1)}, bf16[576,768]{1,0:T(8,128)(2,1)}, bf16[576,768]{1,0:T(8,128)(2,1)})) %all-reduce.5.cloned.1.call-update) | async-done | bytes 2654224 | tf_op jit(solution)/shard_map/psum | solution.py:70
  149.7 3.3 %fusion.11 = f32[576,1024]{1,0:T(8,128)S(1)} fusion(bf16[1,1024,768]{2,1,0:T(8,128)(2,1)S(1)} %copy-done, bf16[576,768]{1,0:T(8,128)(2,1)} %get-tuple-element.4, bf16[576,768]{1,0:T(8,128)(2,1)} %get-tuple-element.5, bf16[576,768]{1,0:T(8,128)(2,1)} %get-tuple-element.6), kind=kOutput, calls=%fused_computation.32 | convolution fusion | flops 911720448 | bytes 6586368 | tf_op jit(solution)/shard_map/dot_general | solution.py:14
  153.1 2.2 %add_convert_fusion = bf16[576,1024]{1,0:T(8,128)(2,1)} fusion(f32[576,1024]{1,0:T(8,128)S(1)} %fusion.11, bf16[1,1024,768]{2,1,0:T(8,128)(2,1)S(1)} %copy-done.4, bf16[576,768]{1,0:T(8,128)(2,1)S(1)} %copy-done.8, bf16[576,768]{1,0:T(8,128)(2,1)S(1)} %copy-done.6), kind=kOutput, calls=%fused_computation.16 | convolution fusion | flops 910688256 | bytes 6881280 | tf_op jit(solution)/shard_map/dot_general | solution.py:14
  155.3 5.5 %all-to-all-start.2 = ((bf16[8,72,1024]{2,1,0:T(8,128)(2,1)}), bf16[8,72,1024]{2,1,0:T(8,128)(2,1)S(1)}, u32[]{:S(2)}, u32[]{:S(2)}) async-start(bf16[8,72,1024]{2,1,0:T(8,128)(2,1)} %bitcast.49), calls=%async_computation.2 | async-start | bytes 2359296 | tf_op jit(solution)/shard_map/all_to_all | solution.py:75
  160.9 4.8 %fusion.22 = bf16[1,768,1024]{2,1,0:T(8,128)(2,1)} fusion(bf16[576,1024]{1,0:T(8,128)(2,1)} %bitcast.48, bf16[576,768]{1,0:T(8,128)(2,1)} %get-tuple-element.4, bf16[576,768]{1,0:T(8,128)(2,1)} %get-tuple-element.6), kind=kOutput, calls=%fused_computation.43 | convolution fusion | flops 914178048 | bytes 4521984 | tf_op jit(solution)/shard_map/dot_general | solution.py:8
  165.7 4.2 %fusion.21 = bf16[1,1024,768]{2,1,0:T(8,128)(2,1)} fusion(bf16[576,1024]{1,0:T(8,128)(2,1)} %bitcast.8, bf16[576,768]{1,0:T(8,128)(2,1)S(1)} %copy-done.9, bf16[576,768]{1,0:T(8,128)(2,1)S(1)} %copy-done.7), kind=kOutput, calls=%fused_computation.42 | convolution fusion | flops 914178048 | bytes 4521984 | tf_op jit(solution)/shard_map/dot_general | solution.py:8
  169.9 4.4 %fusion.20 = bf16[1,1024,768]{2,1,0:T(8,128)(2,1)} fusion(bf16[576,1024]{1,0:T(8,128)(2,1)} %bitcast.8, bf16[576,768]{1,0:T(8,128)(2,1)S(1)} %copy-done.5, bf16[576,768]{1,0:T(8,128)(2,1)S(1)} %copy-done.7, bf16[576,768]{1,0:T(8,128)(2,1)S(1)} %copy-done.9), kind=kOutput, calls=%fused_computation.41 | convolution fusion | flops 916389888 | bytes 5406720 | tf_op jit(solution)/shard_map/dot_general | solution.py:8
  174.3 14.9 %all-to-all-done.2 = bf16[8,72,1024]{2,1,0:T(8,128)(2,1)S(1)} async-done(((bf16[8,72,1024]{2,1,0:T(8,128)(2,1)}), bf16[8,72,1024]{2,1,0:T(8,128)(2,1)S(1)}, u32[]{:S(2)}, u32[]{:S(2)}) %all-to-all-start.2) | async-done | bytes 1179680 | tf_op jit(solution)/shard_map/all_to_all | solution.py:75
  189.2 2.8 %gather_fusion.3 = bf16[512,1024]{1,0:T(8,128)(2,1)} fusion(bf16[576,1024]{1,0:T(8,128)(2,1)S(1)} %bitcast.45, s32[1024]{0:T(1024)S(1)} %pad_clamp_fusion), kind=kCustom, calls=%fused_computation.3 | custom fusion | bytes 2099200 | tf_op jit(solution)/shard_map/gather | solution.py:87
  191.9 1.5 gather.18
  193.4 2.1 %reduce_sum.25 = bf16[128,1024]{1,0:T(8,128)(2,1)} reduce(bf16[128,4,1024]{2,1,0:T(4,128)(2,1)S(1)} %gather.18, bf16[]{:T(256)} %constant.14.clone.1), dimensions={1}, to_apply=%region_7.8 | reduce | flops 393216 | bytes 1310722 | tf_op jit(solution)/shard_map/reduce_sum | solution.py:88
  (36 shorter events, 0.6 us)
Async XLA Ops:
  7.2 54.0 %copy-start = (bf16[1,1024,768]{2,1,0:T(8,128)(2,1)S(1)}, bf16[1,1024,768]{2,1,0:T(8,128)(2,1)}, u32[]{:S(2)}) copy-start(bf16[1,1024,768]{2,1,0:T(8,128)(2,1)} %param.11) | copy-start | bytes 4718596
  17.6 7.4 %copy-start.2 = (bf16[128,1024]{1,0:T(8,128)(2,1)S(1)}, bf16[128,1024]{1,0:T(8,128)(2,1)}, u32[]{:S(2)}) copy-start(bf16[128,1024]{1,0:T(8,128)(2,1)} %param.8) | copy-start | bytes 786436
  17.6 36.1 %all-to-all-start.1 = ((bf16[8,72,1024]{2,1,0:T(8,128)(2,1)}), bf16[8,72,1024]{2,1,0:T(8,128)(2,1)}, u32[]{:S(2)}, u32[]{:S(2)}) async-start(bf16[8,72,1024]{2,1,0:T(8,128)(2,1)} %bitcast.7), calls=%async_computation.1 | async-start | bytes 2359296 | tf_op jit(solution)/shard_map/all_to_all | solution.py:60
  25.1 2.9 %copy-start.3 = (f32[128,4]{0,1:T(4,128)S(1)}, f32[128,4]{0,1:T(4,128)}, u32[]{:S(2)}) copy-start(f32[128,4]{0,1:T(4,128)} %param.10) | copy-start | bytes 6148
  53.8 32.4 %all-to-all-start = ((bf16[8,72,1024]{2,1,0:T(8,128)(2,1)}), bf16[8,72,1024]{2,1,0:T(8,128)(2,1)S(1)}, u32[]{:S(2)}, u32[]{:S(2)}) async-start(bf16[8,72,1024]{2,1,0:T(8,128)(2,1)} %fusion), calls=%async_computation | async-start | bytes 2359296 | tf_op jit(solution)/shard_map/all_to_all | solution.py:61
  57.4 92.3 %all-reduce.5.cloned.1.call-start = ((), (), s32[]{:S(2)}) async-start(), calls=%async_computation.3 | async-start | bytes 5308416 | tf_op jit(solution)/shard_map/psum | solution.py:70
  86.1 3.9 %copy-start.1 = (bf16[8,72,1024]{2,1,0:T(8,128)(2,1)}, bf16[8,72,1024]{2,1,0:T(8,128)(2,1)S(1)}, u32[]{:S(2)}) copy-start(bf16[8,72,1024]{2,1,0:T(8,128)(2,1)S(1)} %all-to-all-done) | copy-start | bytes 3538948
  149.7 3.3 %copy-start.4 = (bf16[1,1024,768]{2,1,0:T(8,128)(2,1)S(1)}, bf16[1,1024,768]{2,1,0:T(8,128)(2,1)}, u32[]{:S(2)}) copy-start(bf16[1,1024,768]{2,1,0:T(8,128)(2,1)} %param.12) | copy-start | bytes 4718596
  149.7 3.4 %copy-start.6 = (bf16[576,768]{1,0:T(8,128)(2,1)S(1)}, bf16[576,768]{1,0:T(8,128)(2,1)}, u32[]{:S(2)}) copy-start(bf16[576,768]{1,0:T(8,128)(2,1)} %get-tuple-element.5) | copy-start | bytes 2654212
  149.7 3.4 %copy-start.8 = (bf16[576,768]{1,0:T(8,128)(2,1)S(1)}, bf16[576,768]{1,0:T(8,128)(2,1)}, u32[]{:S(2)}) copy-start(bf16[576,768]{1,0:T(8,128)(2,1)} %get-tuple-element.6) | copy-start | bytes 2654212
  155.3 33.8 %all-to-all-start.2 = ((bf16[8,72,1024]{2,1,0:T(8,128)(2,1)}), bf16[8,72,1024]{2,1,0:T(8,128)(2,1)S(1)}, u32[]{:S(2)}, u32[]{:S(2)}) async-start(bf16[8,72,1024]{2,1,0:T(8,128)(2,1)} %bitcast.49), calls=%async_computation.2 | async-start | bytes 2359296 | tf_op jit(solution)/shard_map/all_to_all | solution.py:75
  160.9 4.9 %copy-start.7 = (bf16[576,768]{1,0:T(8,128)(2,1)S(1)}, bf16[576,768]{1,0:T(8,128)(2,1)}, u32[]{:S(2)}) copy-start(bf16[576,768]{1,0:T(8,128)(2,1)} %get-tuple-element.5) | copy-start | bytes 2654212
  160.9 4.9 %copy-start.9 = (bf16[576,768]{1,0:T(8,128)(2,1)S(1)}, bf16[576,768]{1,0:T(8,128)(2,1)}, u32[]{:S(2)}) copy-start(bf16[576,768]{1,0:T(8,128)(2,1)} %get-tuple-element.6) | copy-start | bytes 2654212
  165.7 4.2 %copy-start.5 = (bf16[576,768]{1,0:T(8,128)(2,1)S(1)}, bf16[576,768]{1,0:T(8,128)(2,1)}, u32[]{:S(2)}) copy-start(bf16[576,768]{1,0:T(8,128)(2,1)} %get-tuple-element.4) | copy-start | bytes 2654212
Sparse Core Ops, SparseCore 0:
  90.2 59.5 all-reduce.4
where the time goes:
time: 203 us; the launch traced here: 202 us
  waiting for transfers between devices  118 us (58%)
  matrix products  29.9 us (15%)
  local copies, waits for them, and re-layouts  18.3 us (9%)
  starting transfers between devices  16.6 us (8%)
  between operations  14.2 us (7%)
  other arithmetic  5.5 us (3%)
    psum x1, waiting for transfers between devices, on_device(): lax.psum(up_part.astype(jnp.bfloat16), 'tp').astype(jnp.float32)  59.7 us
    all_to_all x1, waiting for transfers between devices, on_device(): lax.all_to_all(send_dy, 'ep', split_axis=0, concat_axis=0, tiled=True)  21.6 us
    all_to_all x1, waiting for transfers between devices, on_device(): lax.all_to_all(send_x, 'ep', split_axis=0, concat_axis=0, tiled=True)  21.6 us
    all_to_all x1, waiting for transfers between devices, on_device(): lax.all_to_all(dx_rows.reshape(experts, capacity, width_part), 'ep', spli...  14.9 us
    dot_general x3, matrix products, contract_rows(): lax.dot_general(left, right, (((0,), (0,)), ((), ())), preferred_element_...  13.4 us
    dot_general x3, matrix products, contract_cols(): lax.dot_general(left, right, (((1,), (1,)), ((), ())), preferred_element_...  9.42 us
    all_to_all x1, starting transfers between devices, on_device(): lax.all_to_all(send_x, 'ep', split_axis=0, concat_axis=0, tiled=True)  7.44 us
    all_to_all x1, starting transfers between devices, on_device(): lax.all_to_all(dx_rows.reshape(experts, capacity, width_part), 'ep', spli...  5.52 us
  transfers between devices with their start and end apart: 4, of which 4 were waited for; matrix products, arithmetic and copies ran while one was open for 14% of the time, Pallas kernels for 0%

commit v1 on v0

--- a/solution.py
+++ b/solution.py
@@ -1,6 +1,10 @@
+import functools
+
 import jax
 import jax.numpy as jnp
 from jax import lax
+from jax.experimental import pallas as pl
+from jax.experimental.pallas import tpu as pltpu
 from jax.sharding import PartitionSpec as P
 
 
@@ -89,6 +93,324 @@
     return (grad_tokens, fisher_gate, fisher_up, fisher_down)
 
 
+MESH = pl.DeviceIdType.MESH
+F32 = jnp.float32
+BF16 = jnp.bfloat16
+ROW_TILE = 16
+LANES = 128
+VMEM_BYTES = 60 * 1024 * 1024
+
+
+def flipped(index, mask):
+    out, bit = index, 1
+    while bit <= mask:
+        if mask & bit:
+            out = out + bit * (1 - 2 * ((index // bit) % 2))
+        bit *= 2
+    return out
+
+
+def slot_rows(tok_rows, top_count, experts):
+    capacity = tok_rows * top_count * 9 // (8 * experts)
+    return -(-capacity // ROW_TILE) * ROW_TILE
+
+
+def fused_kernel(
+    n_ep, n_tp, rows,
+    tok_ref, og_ref, pe_ref, wg_hbm, wu_hbm, wd_hbm,
+    grad_ref, fg_hbm, fu_hbm, fd_hbm,
+    wg, wu, wd, rank, onehot, sx, rx, pb, rb, af, dxs, ret, tsq, sqb, fg, fu, fd,
+    w_sem, o_sem, xs_sem, xr_sem, ps_sem, pr_sem, as_sem, ar_sem, ds_sem, dr_sem,
+):
+    e = lax.axis_index("ep")
+    q = lax.axis_index("tp")
+    tok_rows, width = tok_ref.shape
+    ff = wg.shape[1]
+    half = ff // 2
+    pair = 2 * rows
+    chunks = n_ep // 2
+    scale = 1.0 / tok_rows
+
+    loads = [
+        pltpu.make_async_copy(hbm.at[0], vmem, w_sem.at[i])
+        for i, (hbm, vmem) in enumerate(((wg_hbm, wg), (wu_hbm, wu), (wd_hbm, wd)))
+    ]
+    for copy in loads:
+        copy.start()
+
+    barrier = pltpu.get_barrier_semaphore()
+    for k in range(1, n_ep):
+        pl.semaphore_signal(barrier, inc=1, device_id=(flipped(e, k), q), device_id_type=MESH)
+    for j in range(1, n_tp):
+        pl.semaphore_signal(barrier, inc=1, device_id=(e, flipped(q, j)), device_id_type=MESH)
+
+    mask = (pe_ref[...] > 0.0).astype(F32)
+    before = (
+        lax.broadcasted_iota(jnp.int32, (tok_rows, tok_rows), 0)
+        < lax.broadcasted_iota(jnp.int32, (tok_rows, tok_rows), 1)
+    ).astype(BF16)
+    ranks = jnp.dot(mask.astype(BF16), before, preferred_element_type=F32)
+    rank[...] = jnp.where(mask > 0.0, ranks, -1.0).astype(jnp.int32)
+    slot_iota = lax.broadcasted_iota(jnp.int32, (rows, tok_rows), 0)
+    pl.semaphore_wait(barrier, n_ep + n_tp - 2)
+
+    def block(k):
+        return pl.ds(k * rows, rows)
+
+    x_copies = [None] * n_ep
+    for k in list(range(1, n_ep)) + [0]:
+        dest = flipped(e, k)
+        hot = (slot_iota == rank[pl.ds(dest, 1), :]).astype(F32)
+        hot16 = hot.astype(BF16)
+        onehot[block(k), :] = hot16
+        xs = jnp.dot(hot16, tok_ref[...], preferred_element_type=F32).astype(BF16)
+        prob = jnp.sum(hot * pe_ref[pl.ds(dest, 1), :], 1, keepdims=True)
+        dys = (jnp.dot(hot16, og_ref[...], preferred_element_type=F32) * prob).astype(BF16)
+        out = rx if k == 0 else sx
+        out[0, block(k), :] = xs
+        out[1, block(k), :] = dys
+        if k:
+            copies = []
+            for i in range(2):
+                copy = pltpu.make_async_remote_copy(
+                    src_ref=sx.at[i, block(k), :],
+                    dst_ref=rx.at[i, block(k), :],
+                    send_sem=xs_sem.at[i, k],
+                    recv_sem=xr_sem.at[i, k],
+                    device_id=(dest, q),
+                    device_id_type=MESH,
+                )
+                copy.start()
+                copies.append(copy)
+            x_copies[k] = copies
+
+    def piece(index):
+        return (
+            pl.ds(pl.multiple_of((index // 2) * rows, ROW_TILE), rows),
+            pl.ds(pl.multiple_of((index % 2) * half, LANES), half),
+        )
+
+    p_copies = [None] * chunks
+    a_copies = [None] * chunks
+    d_copies = [None] * n_ep
+
+    def partials(c):
+        span = pl.ds(c * pair, pair)
+        for k in (2 * c, 2 * c + 1):
+            if k:
+                x_copies[k][0].wait_recv()
+        if c == 0:
+            loads[0].wait()
+            loads[1].wait()
+        x = rx[0, span, :]
+        pb[c, 0] = jnp.dot(x, wg[...], preferred_element_type=F32).astype(BF16)
+        pb[c, 1] = jnp.dot(x, wu[...], preferred_element_type=F32).astype(BF16)
+        for k in (2 * c, 2 * c + 1):
+            if k:
+                x_copies[k][1].wait_recv()
+        if c == 0:
+            loads[2].wait()
+        pb[c, 2] = contract_cols(rx[1, span, :], wd[...]).astype(BF16)
+        p_copies[c] = []
+        for j in range(1, n_tp):
+            other = flipped(q, j)
+            r, l = piece(other)
+            copy = pltpu.make_async_remote_copy(
+                src_ref=pb.at[c, :, r, l],
+                dst_ref=rb.at[c, j - 1],
+                send_sem=ps_sem.at[c, j],
+                recv_sem=pr_sem.at[c, j],
+                device_id=(e, other),
+                device_id_type=MESH,
+            )
+            copy.start()
+            p_copies[c].append(copy)
+
+    def activate(c):
+        for copy in p_copies[c]:
+            copy.wait_recv()
+        r, l = piece(q)
+        gate, up, dact = [
+            pb[c, i, r, l].astype(F32)
+            + rb[c, 0, i].astype(F32)
+            + rb[c, 1, i].astype(F32)
+            + rb[c, 2, i].astype(F32)
+            for i in range(3)
+        ]
+        r = pl.ds(pl.multiple_of(c * pair + (q // 2) * rows, ROW_TILE), rows)
+        for i, value in enumerate(swiglu_back(gate, up, dact)):
+            af[i, r, l] = value
+        a_copies[c] = []
+        for j in range(1, n_tp):
+            copy = pltpu.make_async_remote_copy(
+                src_ref=af.at[:, r, l],
+                dst_ref=af.at[:, r, l],
+                send_sem=as_sem.at[c, j],
+                recv_sem=ar_sem.at[c, j],
+                device_id=(e, flipped(q, j)),
+                device_id_type=MESH,
+            )
+            copy.start()
+            a_copies[c].append(copy)
+
+    def input_grad(c):
+        for j, copy in enumerate(a_copies[c]):
+            r, l = piece(flipped(q, j + 1))
+            r = pl.ds(
+                pl.multiple_of(c * pair + (flipped(q, j + 1) // 2) * rows, ROW_TILE), rows
+            )
+            pltpu.make_async_remote_copy(
+                src_ref=af.at[:, r, l],
+                dst_ref=af.at[:, r, l],
+                send_sem=as_sem.at[c, j + 1],
+                recv_sem=ar_sem.at[c, j + 1],
+                device_id=(e, flipped(q, j + 1)),
+                device_id_type=MESH,
+            ).wait_recv()
+        span = pl.ds(c * pair, pair)
+        dx = contract_cols(af[1, span, :], wg[...]) + contract_cols(af[2, span, :], wu[...])
+        dxs[span, :] = dx.astype(BF16)
+        for k in (2 * c, 2 * c + 1):
+            if k:
+                copy = pltpu.make_async_remote_copy(
+                    src_ref=dxs.at[block(k), :],
+                    dst_ref=ret.at[block(k), :],
+                    send_sem=ds_sem.at[k],
+                    recv_sem=dr_sem.at[k],
+                    device_id=(flipped(e, k), q),
+                    device_id_type=MESH,
+                )
+                copy.start()
+                d_copies[k] = copy
+            else:
+                ret[block(0), :] = dxs[block(0), :]
+
+    for c in range(chunks + 2):
+        if c < chunks:
+            partials(c)
+        if 0 < c <= chunks:
+            activate(c - 1)
+        if c > 1:
+            input_grad(c - 2)
+    def transposed_squares(source, i, columns):
+        @pl.loop(0, columns // LANES)
+        def _(step):
+            l = pl.ds(pl.multiple_of(step * LANES, LANES), LANES)
+            tsq[l, :] = squared(source[i, :, l]).T
+
+    def fisher(columns, depth, out):
+        @pl.loop(0, columns // LANES)
+        def _(step):
+            r = pl.ds(pl.multiple_of(step * LANES, LANES), LANES)
+            sums = jnp.dot(tsq[r, :], sqb[:, :depth], preferred_element_type=F32)
+            out[r, :] = (sums * scale).astype(BF16)
+
+    stores = []
+
+    def store(i, vmem, hbm):
+        copy = pltpu.make_async_copy(vmem, hbm.at[0], o_sem.at[i])
+        copy.start()
+        stores.append(copy)
+
+    transposed_squares(rx, 0, width)
+    sqb[:, :ff] = squared(af[1])
+    fisher(width, ff, fg)
+    store(0, fg, fg_hbm)
+    sqb[:, :ff] = squared(af[2])
+    fisher(width, ff, fu)
+    store(1, fu, fu_hbm)
+    transposed_squares(af, 0, ff)
+    sqb[...] = squared(rx[1])
+    fisher(ff, width, fd)
+    store(2, fd, fd_hbm)
+
+    for k in range(1, n_ep):
+        d_copies[k].wait_recv()
+    grad_ref[...] = contract_rows(onehot[...], ret[...]).astype(BF16)
+
+    for k in range(1, n_ep):
+        for copy in x_copies[k]:
+            copy.wait_send()
+        d_copies[k].wait_send()
+    for c in range(chunks):
+        for copy in p_copies[c] + a_copies[c]:
+            copy.wait_send()
+    for copy in stores:
+        copy.wait()
+
+
+def fused_on_device(n_ep, n_tp, tokens, out_grad, expert_ids, route_probs, w_gate, w_up, w_down):
+    tok_rows, width = tokens.shape
+    ff = w_gate.shape[2]
+    rows = slot_rows(tok_rows, expert_ids.shape[1], n_ep)
+    total, chunks = n_ep * rows, n_ep // 2
+    names = jnp.arange(n_ep, dtype=jnp.int32)[:, None, None]
+    probs = jnp.sum(jnp.where(expert_ids[None] == names, route_probs[None], 0.0), 2)
+    any_spec = pl.BlockSpec(memory_space=pl.ANY)
+    vmem_spec = pl.BlockSpec(memory_space=pltpu.VMEM)
+    dma = pltpu.SemaphoreType.DMA
+    return pl.pallas_call(
+        functools.partial(fused_kernel, n_ep, n_tp, rows),
+        out_shape=(
+            jax.ShapeDtypeStruct(tokens.shape, BF16),
+            jax.ShapeDtypeStruct(w_gate.shape, BF16),
+            jax.ShapeDtypeStruct(w_up.shape, BF16),
+            jax.ShapeDtypeStruct(w_down.shape, BF16),
+        ),
+        in_specs=[vmem_spec] * 3 + [any_spec] * 3,
+        out_specs=[vmem_spec] + [any_spec] * 3,
+        scratch_shapes=[
+            pltpu.VMEM((width, ff), BF16),
+            pltpu.VMEM((width, ff), BF16),
+            pltpu.VMEM((ff, width), BF16),
+            pltpu.VMEM((n_ep, tok_rows), jnp.int32),
+            pltpu.VMEM((total, tok_rows), BF16),
+            pltpu.VMEM((2, total, width), BF16),
+            pltpu.VMEM((2, total, width), BF16),
+            pltpu.VMEM((chunks, 3, 2 * rows, ff), BF16),
+            pltpu.VMEM((chunks, n_tp - 1, 3, rows, ff // 2), BF16),
+            pltpu.VMEM((3, total, ff), BF16),
+            pltpu.VMEM((total, width), BF16),
+            pltpu.VMEM((total, width), BF16),
+            pltpu.VMEM((width, total), BF16),
+            pltpu.VMEM((total, width), BF16),
+            pltpu.VMEM((width, ff), BF16),
+            pltpu.VMEM((width, ff), BF16),
+            pltpu.VMEM((ff, width), BF16),
+            dma((3,)),
+            dma((3,)),
+            dma((2, n_ep)),
+            dma((2, n_ep)),
+            dma((chunks, n_tp)),
+            dma((chunks, n_tp)),
+            dma((chunks, n_tp)),
+            dma((chunks, n_tp)),
+            dma((n_ep,)),
+            dma((n_ep,)),
+        ],
+        compiler_params=pltpu.CompilerParams(
+            collective_id=0, has_side_effects=True, vmem_limit_bytes=VMEM_BYTES
+        ),
+    )(tokens, out_grad, probs, w_gate, w_up, w_down)
+
+
+def part(n_ep, n_tp, *args):
+    tokens, expert_ids, w_gate = args[0], args[2], args[4]
+    width, ff = w_gate.shape[1:]
+    rows = slot_rows(tokens.shape[0], expert_ids.shape[1], n_ep)
+    fits = (
+        n_tp == 4
+        and n_ep in (2, 4, 8)
+        and ff <= width
+        and ff % (2 * LANES) == 0
+        and width % LANES == 0
+        and n_ep * rows * (17 * width + 18 * ff) + 14 * width * ff < VMEM_BYTES
+    )
+    if fits:
+        return fused_on_device(n_ep, n_tp, *args)
+    return on_device(*args)
+
+
 def solution(mesh):
     in_specs = (
         P("ep", "tp"),
@@ -101,5 +423,5 @@
     )
     out_specs = (P("ep", "tp"), P("ep", "tp", None), P("ep", "tp", None), P("ep", None, "tp"))
     return jax.shard_map(
-        on_device, mesh=mesh, in_specs=in_specs, out_specs=out_specs, check_vma=False
-    )
+        functools.partial(part, mesh.shape["ep"], mesh.shape["tp"]), mesh=mesh, in_specs=in_specs, out_specs=out_specs, check_vma=False
+    )

time: 203 us -> 124 us (0.61)
  the two profiles are of different devices: /device:TPU:0 before, /device:TPU:9 now
where the time goes in v1:
time: 124 us
  Pallas kernels  114 us (92%)
  local copies, waits for them, and re-layouts  7.56 us (6%)
  other arithmetic  1.3 us (1%)
    pallas_call x1, Pallas kernels, fused_on_device(): pl.pallas_call(functools.partial(fused_kernel, n_ep, n_tp, rows), out_sha...  114 us
    unnamed x8, local copies, waits for them, and re-layouts  7.56 us

profile of v1, /device:TPU:9, one launch (start us, length us, event | category | flops | bytes accessed | tf_op | source)
XLA Modules:
  0.0 123.9 jit_solution(5892441574523782945)
XLA Ops:
  0.6 1.3 %select_reduce_fusion.pe_ref = f32[8,128]{1,0:T(8,128)} fusion(f32[128,4]{0,1:T(4,128)} %param.10, s32[128,4]{0,1:T(4,128)} %param.9), kind=kLoop, calls=%fused_computation | loop fusion | flops 11264 | bytes 8192 | tf_op jit(solution)/shard_map/reduce_sum | solution.py:348
  1.9 114.4 %shard_map.102 = (bf16[128,1024]{1,0:T(8,128)(2,1)}, bf16[1,1024,768]{2,1,0:T(8,128)(2,1)}, bf16[1,1024,768]{2,1,0:T(8,128)(2,1)}, bf16[1,768,1024]{2,1,0:T(8,128)(2,1)}) custom-call(bf16[128,1024]{1,0:T(8,128)(2,1)} %tok_ref.1, bf16[128,1024]{1,0:T(8,128)(2,1)} %og_ref.1, f32[8,128]{1,0:T(8,128)} %select_reduce_fusion.pe_ref, bf16[1,1024,768]{2,1,0:T(8,128)(2,1)} %wg_hbm.1, ...), custom_call_target="tpu_custom_call" | custom-call | tf_op jit(solution)/shard_map/pallas_call | solution.py:352
  116.3 1.7 %copy.17 = bf16[128,1024]{1,0:T(8,128)(2,1)} copy(bf16[128,1024]{1,0:T(8,128)(2,1)} %get-tuple-element.8) | data formatting | bytes 524288
  118.0 0.0 copy-start.1
  118.0 2.8 %copy.18 = bf16[1,1024,768]{2,1,0:T(8,128)(2,1)} copy(bf16[1,1024,768]{2,1,0:T(8,128)(2,1)} %get-tuple-element.9) | data formatting | bytes 3145728
  120.8 0.0 copy-done.1
  120.8 0.0 copy-start
  120.8 1.1 copy.19
  121.9 0.8 copy-done
  122.7 1.1 copy.20
Async XLA Ops:
  118.0 2.8 %copy-start.1 = (bf16[1,1024,768]{2,1,0:T(8,128)(2,1)S(1)}, bf16[1,1024,768]{2,1,0:T(8,128)(2,1)}, u32[]{:S(2)}) copy-start(bf16[1,1024,768]{2,1,0:T(8,128)(2,1)} %get-tuple-element.10) | copy-start | bytes 4718596
  120.8 2.0 %copy-start = (bf16[1,768,1024]{2,1,0:T(8,128)(2,1)S(1)}, bf16[1,768,1024]{2,1,0:T(8,128)(2,1)}, u32[]{:S(2)}) copy-start(bf16[1,768,1024]{2,1,0:T(8,128)(2,1)} %get-tuple-element.11) | copy-start | bytes 4718596

commit v2 on v1

--- a/solution.py
+++ b/solution.py
@@ -119,17 +119,20 @@
     n_ep, n_tp, rows,
     tok_ref, og_ref, pe_ref, wg_hbm, wu_hbm, wd_hbm,
     grad_ref, fg_hbm, fu_hbm, fd_hbm,
-    wg, wu, wd, rank, onehot, sx, rx, pb, rb, af, dxs, ret, tsq, sqb, fg, fu, fd,
-    w_sem, o_sem, xs_sem, xr_sem, ps_sem, pr_sem, as_sem, ar_sem, ds_sem, dr_sem,
+    wg, wu, wd, rank, onehot, peb, tb, sx, rx, pb, rb, sb, rb2, af, dxs, ret, tsq, sqb, fg, fu, fd,
+    w_sem, o_sem, pes_sem, per_sem, ts_sem, tr_sem, xs_sem, xr_sem,
+    ps_sem, pr_sem, qs_sem, qr_sem, as_sem, ar_sem, ds_sem, dr_sem,
 ):
     e = lax.axis_index("ep")
     q = lax.axis_index("tp")
+    row, mate = e // 2, flipped(e, 1)
     tok_rows, width = tok_ref.shape
     ff = wg.shape[1]
     half = ff // 2
     pair = 2 * rows
     chunks = n_ep // 2
     scale = 1.0 / tok_rows
+    blocks = (tok_ref, og_ref)
 
     loads = [
         pltpu.make_async_copy(hbm.at[0], vmem, w_sem.at[i])
@@ -143,46 +146,121 @@
         pl.semaphore_signal(barrier, inc=1, device_id=(flipped(e, k), q), device_id_type=MESH)
     for j in range(1, n_tp):
         pl.semaphore_signal(barrier, inc=1, device_id=(e, flipped(q, j)), device_id_type=MESH)
-
-    mask = (pe_ref[...] > 0.0).astype(F32)
     before = (
         lax.broadcasted_iota(jnp.int32, (tok_rows, tok_rows), 0)
         < lax.broadcasted_iota(jnp.int32, (tok_rows, tok_rows), 1)
     ).astype(BF16)
-    ranks = jnp.dot(mask.astype(BF16), before, preferred_element_type=F32)
-    rank[...] = jnp.where(mask > 0.0, ranks, -1.0).astype(jnp.int32)
     slot_iota = lax.broadcasted_iota(jnp.int32, (rows, tok_rows), 0)
     pl.semaphore_wait(barrier, n_ep + n_tp - 2)
 
+    def remote(src, dst, send_sem, recv_sem, device):
+        return pltpu.make_async_remote_copy(
+            src_ref=src,
+            dst_ref=dst,
+            send_sem=send_sem,
+            recv_sem=recv_sem,
+            device_id=device,
+            device_id_type=MESH,
+        )
+
     def block(k):
         return pl.ds(k * rows, rows)
 
-    x_copies = [None] * n_ep
-    for k in list(range(1, n_ep)) + [0]:
-        dest = flipped(e, k)
-        hot = (slot_iota == rank[pl.ds(dest, 1), :]).astype(F32)
-        hot16 = hot.astype(BF16)
-        onehot[block(k), :] = hot16
-        xs = jnp.dot(hot16, tok_ref[...], preferred_element_type=F32).astype(BF16)
-        prob = jnp.sum(hot * pe_ref[pl.ds(dest, 1), :], 1, keepdims=True)
-        dys = (jnp.dot(hot16, og_ref[...], preferred_element_type=F32) * prob).astype(BF16)
-        out = rx if k == 0 else sx
-        out[0, block(k), :] = xs
-        out[1, block(k), :] = dys
-        if k:
-            copies = []
-            for i in range(2):
-                copy = pltpu.make_async_remote_copy(
-                    src_ref=sx.at[i, block(k), :],
-                    dst_ref=rx.at[i, block(k), :],
-                    send_sem=xs_sem.at[i, k],
-                    recv_sem=xr_sem.at[i, k],
-                    device_id=(dest, q),
-                    device_id_type=MESH,
+    def hop(direction, distance, i):
+        step = 1 - 2 * direction
+        source = row - step * distance
+        src = blocks[i] if distance == 0 else tb.at[source, i]
+        return remote(
+            src,
+            tb.at[source, i],
+            ts_sem.at[direction, distance, i],
+            tr_sem.at[direction, distance, i],
+            (e + 2 * step, q),
+        )
+
+    def sends(direction, distance):
+        if direction == 0:
+            return (row >= distance) & (row < chunks - 1)
+        return (row + distance < chunks) & (row > 0)
+
+    def holds(direction, distance):
+        if direction == 0:
+            return row >= distance
+        return row + distance < chunks
+
+    def landed(direction, distance, i):
+        source = row - (1 - 2 * direction) * distance
+        return remote(
+            tb.at[source, i],
+            tb.at[source, i],
+            ts_sem.at[direction, distance - 1, i],
+            tr_sem.at[direction, distance - 1, i],
+            (mate, q),
+        )
+
+    def arrive(distance):
+        for i in range(2):
+            for direction in range(2):
+                if distance:
+
+                    @pl.when(holds(direction, distance))
+                    def _():
+                        landed(direction, distance, i).wait_recv()
+
+                if distance < chunks - 1:
+
+                    @pl.when(sends(direction, distance))
+                    def _():
+                        hop(direction, distance, i).start()
+
+    pe_copies = [None] * chunks
+
+    def send_probs():
+        for c in range(1, chunks):
+            pe_copies[c] = remote(
+                pe_ref, peb.at[row], pes_sem.at[c], per_sem.at[c], (flipped(e, 2 * c), q)
+            )
+            pe_copies[c].start()
+
+    def ranked(probs):
+        mask = (probs > 0.0).astype(F32)
+        ranks = jnp.dot(mask.astype(BF16), before, preferred_element_type=F32)
+        rank[...] = jnp.where(mask > 0.0, ranks, -1.0).astype(jnp.int32)
+
+    x_copies = [None] * chunks
+
+    def select(c):
+        source = flipped(row, c)
+        if c:
+            pe_copies[c].wait_recv()
+            probs, pair_of = peb.at[source], (tb.at[source, 0], tb.at[source, 1])
+        else:
+            probs, pair_of = pe_ref, blocks
+        ranked(probs[...])
+        for dest, out, k in ((mate, sx, c), (e, rx, 2 * c)):
+            hot = (slot_iota == rank[pl.ds(dest, 1), :]).astype(F32)
+            hot16 = hot.astype(BF16)
+            prob = jnp.sum(hot * probs[pl.ds(dest, 1), :], 1, keepdims=True)
+            out[0, block(k), :] = jnp.dot(
+                hot16, pair_of[0][...], preferred_element_type=F32
+            ).astype(BF16)
+            out[1, block(k), :] = (
+                jnp.dot(hot16, pair_of[1][...], preferred_element_type=F32) * prob
+            ).astype(BF16)
+            if out is sx:
+                x_copies[c] = remote(
+                    sx.at[:, block(c), :],
+                    rx.at[:, block(2 * c + 1), :],
+                    xs_sem.at[c],
+                    xr_sem.at[c],
+                    (mate, q),
                 )
-                copy.start()
-                copies.append(copy)
-            x_copies[k] = copies
+                x_copies[c].start()
+
+    def own_onehot():
+        ranked(pe_ref[...])
+        for k in range(n_ep):
+            onehot[block(k), :] = (slot_iota == rank[pl.ds(flipped(e, k), 1), :]).astype(F32).astype(BF16)
 
     def piece(index):
         return (
@@ -190,108 +268,93 @@
             pl.ds(pl.multiple_of((index % 2) * half, LANES), half),
         )
 
+    def placed(c, index):
+        r = pl.ds(pl.multiple_of(c * pair + (index // 2) * rows, ROW_TILE), rows)
+        return af.at[:, r, piece(index)[1]]
+
+    near, far = flipped(q, 1), flipped(q, 2)
     p_copies = [None] * chunks
+    q_copies = [None] * chunks
     a_copies = [None] * chunks
     d_copies = [None] * n_ep
 
     def partials(c):
         span = pl.ds(c * pair, pair)
-        for k in (2 * c, 2 * c + 1):
-            if k:
-                x_copies[k][0].wait_recv()
+        x_copies[c].wait_recv()
         if c == 0:
-            loads[0].wait()
-            loads[1].wait()
+            for copy in loads:
+                copy.wait()
         x = rx[0, span, :]
         pb[c, 0] = jnp.dot(x, wg[...], preferred_element_type=F32).astype(BF16)
         pb[c, 1] = jnp.dot(x, wu[...], preferred_element_type=F32).astype(BF16)
-        for k in (2 * c, 2 * c + 1):
-            if k:
-                x_copies[k][1].wait_recv()
-        if c == 0:
-            loads[2].wait()
         pb[c, 2] = contract_cols(rx[1, span, :], wd[...]).astype(BF16)
         p_copies[c] = []
-        for j in range(1, n_tp):
-            other = flipped(q, j)
+        for j, other in enumerate((near, flipped(q, 3))):
             r, l = piece(other)
-            copy = pltpu.make_async_remote_copy(
-                src_ref=pb.at[c, :, r, l],
-                dst_ref=rb.at[c, j - 1],
-                send_sem=ps_sem.at[c, j],
-                recv_sem=pr_sem.at[c, j],
-                device_id=(e, other),
-                device_id_type=MESH,
+            copy = remote(
+                pb.at[c, :, r, l],
+                rb.at[c, j],
+                ps_sem.at[c, j],
+                pr_sem.at[c, j],
+                (e, near),
             )
             copy.start()
             p_copies[c].append(copy)
 
+    def pair_sum(c):
+        p_copies[c][1].wait_recv()
+        r, l = piece(far)
+        for i in range(3):
+            sb[c, i] = (pb[c, i, r, l].astype(F32) + rb[c, 1, i].astype(F32)).astype(BF16)
+        q_copies[c] = remote(sb.at[c], rb2.at[c], qs_sem.at[c], qr_sem.at[c], (e, far))
+        q_copies[c].start()
+
     def activate(c):
-        for copy in p_copies[c]:
-            copy.wait_recv()
+        p_copies[c][0].wait_recv()
+        q_copies[c].wait_recv()
         r, l = piece(q)
         gate, up, dact = [
-            pb[c, i, r, l].astype(F32)
-            + rb[c, 0, i].astype(F32)
-            + rb[c, 1, i].astype(F32)
-            + rb[c, 2, i].astype(F32)
+            pb[c, i, r, l].astype(F32) + rb[c, 0, i].astype(F32) + rb2[c, i].astype(F32)
             for i in range(3)
         ]
         r = pl.ds(pl.multiple_of(c * pair + (q // 2) * rows, ROW_TILE), rows)
         for i, value in enumerate(swiglu_back(gate, up, dact)):
             af[i, r, l] = value
-        a_copies[c] = []
-        for j in range(1, n_tp):
-            copy = pltpu.make_async_remote_copy(
-                src_ref=af.at[:, r, l],
-                dst_ref=af.at[:, r, l],
-                send_sem=as_sem.at[c, j],
-                recv_sem=ar_sem.at[c, j],
-                device_id=(e, flipped(q, j)),
-                device_id_type=MESH,
-            )
+        mine = placed(c, q)
+        a_copies[c] = [
+            remote(mine, mine, as_sem.at[c, j], ar_sem.at[c, j], (e, other))
+            for j, other in enumerate((far, near))
+        ]
+        for copy in a_copies[c]:
             copy.start()
-            a_copies[c].append(copy)
+
+    def relay(c):
+        theirs = placed(c, far)
+        remote(theirs, theirs, as_sem.at[c, 0], ar_sem.at[c, 0], (e, far)).wait_recv()
+        copy = remote(theirs, theirs, as_sem.at[c, 2], ar_sem.at[c, 2], (e, near))
+        copy.start()
+        a_copies[c].append(copy)
 
     def input_grad(c):
-        for j, copy in enumerate(a_copies[c]):
-            r, l = piece(flipped(q, j + 1))
-            r = pl.ds(
-                pl.multiple_of(c * pair + (flipped(q, j + 1) // 2) * rows, ROW_TILE), rows
-            )
-            pltpu.make_async_remote_copy(
-                src_ref=af.at[:, r, l],
-                dst_ref=af.at[:, r, l],
-                send_sem=as_sem.at[c, j + 1],
-                recv_sem=ar_sem.at[c, j + 1],
-                device_id=(e, flipped(q, j + 1)),
-                device_id_type=MESH,
-            ).wait_recv()
+        for j, index in ((1, near), (2, flipped(q, 3))):
+            theirs = placed(c, index)
+            remote(theirs, theirs, as_sem.at[c, j], ar_sem.at[c, j], (e, near)).wait_recv()
         span = pl.ds(c * pair, pair)
         dx = contract_cols(af[1, span, :], wg[...]) + contract_cols(af[2, span, :], wu[...])
         dxs[span, :] = dx.astype(BF16)
         for k in (2 * c, 2 * c + 1):
             if k:
-                copy = pltpu.make_async_remote_copy(
-                    src_ref=dxs.at[block(k), :],
-                    dst_ref=ret.at[block(k), :],
-                    send_sem=ds_sem.at[k],
-                    recv_sem=dr_sem.at[k],
-                    device_id=(flipped(e, k), q),
-                    device_id_type=MESH,
+                d_copies[k] = remote(
+                    dxs.at[block(k), :],
+                    ret.at[block(k), :],
+                    ds_sem.at[k],
+                    dr_sem.at[k],
+                    (flipped(e, k), q),
                 )
-                copy.start()
-                d_copies[k] = copy
+                d_copies[k].start()
             else:
                 ret[block(0), :] = dxs[block(0), :]
 
-    for c in range(chunks + 2):
-        if c < chunks:
-            partials(c)
-        if 0 < c <= chunks:
-            activate(c - 1)
-        if c > 1:
-            input_grad(c - 2)
     def transposed_squares(source, i, columns):
         @pl.loop(0, columns // LANES)
         def _(step):
@@ -312,7 +375,25 @@
         copy.start()
         stores.append(copy)
 
+    arrive(0)
+    send_probs()
+    for c in range(chunks):
+        if c:
+            arrive(c)
+            activate(c - 1)
+        select(c)
+        partials(c)
+        if c:
+            relay(c - 1)
+        pair_sum(c)
+        if c:
+            input_grad(c - 1)
+    last = chunks - 1
     transposed_squares(rx, 0, width)
+    activate(last)
+    relay(last)
+    own_onehot()
+    input_grad(last)
     sqb[:, :ff] = squared(af[1])
     fisher(width, ff, fg)
     store(0, fg, fg_hbm)
@@ -328,13 +409,16 @@
         d_copies[k].wait_recv()
     grad_ref[...] = contract_rows(onehot[...], ret[...]).astype(BF16)
 
-    for k in range(1, n_ep):
-        for copy in x_copies[k]:
-            copy.wait_send()
-        d_copies[k].wait_send()
-    for c in range(chunks):
-        for copy in p_copies[c] + a_copies[c]:
-            copy.wait_send()
+    for distance in range(chunks - 1):
+        for direction in range(2):
+
+            @pl.when(sends(direction, distance))
+            def _():
+                for i in range(2):
+                    hop(direction, distance, i).wait_send()
+
+    for copy in pe_copies[1:] + x_copies + q_copies + d_copies[1:] + sum(p_copies + a_copies, []):
+        copy.wait_send()
     for copy in stores:
         copy.wait()
 
@@ -365,10 +449,14 @@
             pltpu.VMEM((ff, width), BF16),
             pltpu.VMEM((n_ep, tok_rows), jnp.int32),
             pltpu.VMEM((total, tok_rows), BF16),
-            pltpu.VMEM((2, total, width), BF16),
+            pltpu.VMEM((chunks, n_ep, tok_rows), F32),
+            pltpu.VMEM((chunks, 2, tok_rows, width), BF16),
+            pltpu.VMEM((2, total // 2, width), BF16),
             pltpu.VMEM((2, total, width), BF16),
             pltpu.VMEM((chunks, 3, 2 * rows, ff), BF16),
-            pltpu.VMEM((chunks, n_tp - 1, 3, rows, ff // 2), BF16),
+            pltpu.VMEM((chunks, 2, 3, rows, ff // 2), BF16),
+            pltpu.VMEM((chunks, 3, rows, ff // 2), BF16),
+            pltpu.VMEM((chunks, 3, rows, ff // 2), BF16),
             pltpu.VMEM((3, total, ff), BF16),
             pltpu.VMEM((total, width), BF16),
             pltpu.VMEM((total, width), BF16),
@@ -379,12 +467,18 @@
             pltpu.VMEM((ff, width), BF16),
             dma((3,)),
             dma((3,)),
-            dma((2, n_ep)),
-            dma((2, n_ep)),
-            dma((chunks, n_tp)),
-            dma((chunks, n_tp)),
-            dma((chunks, n_tp)),
-            dma((chunks, n_tp)),
+            dma((chunks,)),
+            dma((chunks,)),
+            dma((2, chunks, 2)),
+            dma((2, chunks, 2)),
+            dma((chunks,)),
+            dma((chunks,)),
+            dma((chunks, 2)),
+            dma((chunks, 2)),
+            dma((chunks,)),
+            dma((chunks,)),
+            dma((chunks, 3)),
+            dma((chunks, 3)),
             dma((n_ep,)),
             dma((n_ep,)),
         ],
@@ -400,7 +494,7 @@
     rows = slot_rows(tokens.shape[0], expert_ids.shape[1], n_ep)
     fits = (
         n_tp == 4
-        and n_ep in (2, 4, 8)
+        and n_ep in (4, 8)
         and ff <= width
         and ff % (2 * LANES) == 0
         and width % LANES == 0

time: 124 us -> 116 us (0.935)
  Pallas kernels: 114 us -> 107 us
    pallas_call x1, Pallas kernels: 114 us -> 107 us  [fused_on_device(): pl.pallas_call(functools.partial(fused_kernel, n_ep, n_tp, rows), out_sha...]
where the time goes in v2:
time: 116 us
  Pallas kernels  107 us (92%)
  local copies, waits for them, and re-layouts  7.56 us (7%)
  other arithmetic  1.3 us (1%)
    pallas_call x1, Pallas kernels, fused_on_device(): pl.pallas_call(functools.partial(fused_kernel, n_ep, n_tp, rows), out_sha...  107 us
    unnamed x8, local copies, waits for them, and re-layouts  7.56 us

profile of v2, /device:TPU:9, one launch (start us, length us, event | category | flops | bytes accessed | tf_op | source)
XLA Modules:
  0.0 116.2 jit_solution(4949084582890598532)
XLA Ops:
  0.6 1.3 %select_reduce_fusion.pe_ref = f32[8,128]{1,0:T(8,128)} fusion(f32[128,4]{0,1:T(4,128)} %param.10, s32[128,4]{0,1:T(4,128)} %param.9), kind=kLoop, calls=%fused_computation | loop fusion | flops 11264 | bytes 8192 | tf_op jit(solution)/shard_map/reduce_sum | solution.py:432
  1.9 106.7 %shard_map.102 = (bf16[128,1024]{1,0:T(8,128)(2,1)}, bf16[1,1024,768]{2,1,0:T(8,128)(2,1)}, bf16[1,1024,768]{2,1,0:T(8,128)(2,1)}, bf16[1,768,1024]{2,1,0:T(8,128)(2,1)}) custom-call(bf16[128,1024]{1,0:T(8,128)(2,1)} %tok_ref.1, bf16[128,1024]{1,0:T(8,128)(2,1)} %og_ref.1, f32[8,128]{1,0:T(8,128)} %select_reduce_fusion.pe_ref, bf16[1,1024,768]{2,1,0:T(8,128)(2,1)} %wg_hbm.1, ...), custom_call_target="tpu_custom_call" | custom-call | tf_op jit(solution)/shard_map/pallas_call | solution.py:436
  108.6 1.7 %copy.17 = bf16[128,1024]{1,0:T(8,128)(2,1)} copy(bf16[128,1024]{1,0:T(8,128)(2,1)} %get-tuple-element.8) | data formatting | bytes 524288
  110.3 0.0 copy-start.1
  110.3 2.8 %copy.18 = bf16[1,1024,768]{2,1,0:T(8,128)(2,1)} copy(bf16[1,1024,768]{2,1,0:T(8,128)(2,1)} %get-tuple-element.9) | data formatting | bytes 3145728
  113.1 0.0 copy-done.1
  113.1 0.0 copy-start
  113.1 1.1 copy.19
  114.2 0.8 copy-done
  115.1 1.1 copy.20
Async XLA Ops:
  110.3 2.8 %copy-start.1 = (bf16[1,1024,768]{2,1,0:T(8,128)(2,1)S(1)}, bf16[1,1024,768]{2,1,0:T(8,128)(2,1)}, u32[]{:S(2)}) copy-start(bf16[1,1024,768]{2,1,0:T(8,128)(2,1)} %get-tuple-element.10) | copy-start | bytes 4718596
  113.1 2.0 %copy-start = (bf16[1,768,1024]{2,1,0:T(8,128)(2,1)S(1)}, bf16[1,768,1024]{2,1,0:T(8,128)(2,1)}, u32[]{:S(2)}) copy-start(bf16[1,768,1024]{2,1,0:T(8,128)(2,1)} %get-tuple-element.11) | copy-start | bytes 4718596

commit v3 on v2

--- a/solution.py
+++ b/solution.py
@@ -98,7 +98,7 @@
 BF16 = jnp.bfloat16
 ROW_TILE = 16
 LANES = 128
-VMEM_BYTES = 60 * 1024 * 1024
+VMEM_BYTES = 36 * 1024 * 1024
 
 
 def flipped(index, mask):
@@ -198,20 +198,19 @@
             (mate, q),
         )
 
-    def arrive(distance):
-        for i in range(2):
-            for direction in range(2):
-                if distance:
-
-                    @pl.when(holds(direction, distance))
-                    def _():
-                        landed(direction, distance, i).wait_recv()
-
-                if distance < chunks - 1:
-
-                    @pl.when(sends(direction, distance))
-                    def _():
-                        hop(direction, distance, i).start()
+    def arrive(distance, i):
+        for direction in range(2):
+            if distance:
+
+                @pl.when(holds(direction, distance))
+                def _():
+                    landed(direction, distance, i).wait_recv()
+
+            if distance < chunks - 1:
+
+                @pl.when(sends(direction, distance))
+                def _():
+                    hop(direction, distance, i).start()
 
     pe_copies = [None] * chunks
 
@@ -227,35 +226,33 @@
         ranks = jnp.dot(mask.astype(BF16), before, preferred_element_type=F32)
         rank[...] = jnp.where(mask > 0.0, ranks, -1.0).astype(jnp.int32)
 
-    x_copies = [None] * chunks
-
-    def select(c):
+    x_copies = [[None, None] for _ in range(chunks)]
+
+    def select(c, i):
         source = flipped(row, c)
         if c:
-            pe_copies[c].wait_recv()
-            probs, pair_of = peb.at[source], (tb.at[source, 0], tb.at[source, 1])
+            if i == 0:
+                pe_copies[c].wait_recv()
+            probs, rows_of = peb.at[source], tb.at[source, i]
         else:
-            probs, pair_of = pe_ref, blocks
-        ranked(probs[...])
+            probs, rows_of = pe_ref, blocks[i]
+        if i == 0:
+            ranked(probs[...])
         for dest, out, k in ((mate, sx, c), (e, rx, 2 * c)):
             hot = (slot_iota == rank[pl.ds(dest, 1), :]).astype(F32)
-            hot16 = hot.astype(BF16)
-            prob = jnp.sum(hot * probs[pl.ds(dest, 1), :], 1, keepdims=True)
-            out[0, block(k), :] = jnp.dot(
-                hot16, pair_of[0][...], preferred_element_type=F32
-            ).astype(BF16)
-            out[1, block(k), :] = (
-                jnp.dot(hot16, pair_of[1][...], preferred_element_type=F32) * prob
-            ).astype(BF16)
+            picked = jnp.dot(hot.astype(BF16), rows_of[...], preferred_element_type=F32)
+            if i:
+                picked = picked * jnp.sum(hot * probs[pl.ds(dest, 1), :], 1, keepdims=True)
+            out[i, block(k), :] = picked.astype(BF16)
             if out is sx:
-                x_copies[c] = remote(
-                    sx.at[:, block(c), :],
-                    rx.at[:, block(2 * c + 1), :],
-                    xs_sem.at[c],
-                    xr_sem.at[c],
+                x_copies[c][i] = remote(
+                    sx.at[i, block(c), :],
+                    rx.at[i, block(2 * c + 1), :],
+                    xs_sem.at[c, i],
+                    xr_sem.at[c, i],
                     (mate, q),
                 )
-                x_copies[c].start()
+                x_copies[c][i].start()
 
     def own_onehot():
         ranked(pe_ref[...])
@@ -280,13 +277,14 @@
 
     def partials(c):
         span = pl.ds(c * pair, pair)
-        x_copies[c].wait_recv()
+        x_copies[c][0].wait_recv()
         if c == 0:
             for copy in loads:
                 copy.wait()
         x = rx[0, span, :]
         pb[c, 0] = jnp.dot(x, wg[...], preferred_element_type=F32).astype(BF16)
         pb[c, 1] = jnp.dot(x, wu[...], preferred_element_type=F32).astype(BF16)
+        x_copies[c][1].wait_recv()
         pb[c, 2] = contract_cols(rx[1, span, :], wd[...]).astype(BF16)
         p_copies[c] = []
         for j, other in enumerate((near, flipped(q, 3))):
@@ -375,13 +373,17 @@
         copy.start()
         stores.append(copy)
 
-    arrive(0)
+    arrive(0, 0)
     send_probs()
+    arrive(0, 1)
     for c in range(chunks):
         if c:
-            arrive(c)
+            arrive(c, 0)
+        select(c, 0)
+        if c:
             activate(c - 1)
-        select(c)
+            arrive(c, 1)
+        select(c, 1)
         partials(c)
         if c:
             relay(c - 1)
@@ -417,7 +419,7 @@
                 for i in range(2):
                     hop(direction, distance, i).wait_send()
 
-    for copy in pe_copies[1:] + x_copies + q_copies + d_copies[1:] + sum(p_copies + a_copies, []):
+    for copy in pe_copies[1:] + q_copies + d_copies[1:] + sum(x_copies + p_copies + a_copies, []):
         copy.wait_send()
     for copy in stores:
         copy.wait()
@@ -471,8 +473,8 @@
             dma((chunks,)),
             dma((2, chunks, 2)),
             dma((2, chunks, 2)),
-            dma((chunks,)),
-            dma((chunks,)),
+            dma((chunks, 2)),
+            dma((chunks, 2)),
             dma((chunks, 2)),
             dma((chunks, 2)),
             dma((chunks,)),

time: 116 us -> 108 us (0.931)
  Pallas kernels: 107 us -> 95.8 us
  local copies, waits for them, and re-layouts: 7.56 us -> 10.3 us
    pallas_call x1, Pallas kernels: 107 us -> 95.8 us  [fused_on_device(): pl.pallas_call(functools.partial(fused_kernel, n_ep, n_tp, rows), out_sha...]
    unnamed x8 -> x14, local copies, waits for them, and re-layouts: 7.56 us -> 10.3 us
where the time goes in v3:
time: 108 us; the launch traced here: 107 us
  Pallas kernels  95.8 us (89%)
  local copies, waits for them, and re-layouts  10.3 us (10%)
    pallas_call x1, Pallas kernels, fused_on_device(): pl.pallas_call(functools.partial(fused_kernel, n_ep, n_tp, rows), out_sha...  95.8 us
    unnamed x14, local copies, waits for them, and re-layouts  10.3 us

profile of v3, /device:TPU:9, one launch (start us, length us, event | category | flops | bytes accessed | tf_op | source)
XLA Modules:
  0.0 107.4 jit_solution(10270278985086553445)
XLA Ops:
  0.6 0.7 select_reduce_fusion.pe_ref
  1.3 0.0 copy-start
  1.3 1.4 %copy-done = bf16[1,1024,768]{2,1,0:T(8,128)(2,1)S(1)} copy-done((bf16[1,1024,768]{2,1,0:T(8,128)(2,1)S(1)}, bf16[1,1024,768]{2,1,0:T(8,128)(2,1)}, u32[]{:S(2)}) %copy-start) | copy-done | bytes 1572888
  2.7 0.0 copy-start.1
  2.8 1.4 %copy-done.1 = bf16[1,1024,768]{2,1,0:T(8,128)(2,1)S(1)} copy-done((bf16[1,1024,768]{2,1,0:T(8,128)(2,1)S(1)}, bf16[1,1024,768]{2,1,0:T(8,128)(2,1)}, u32[]{:S(2)}) %copy-start.1) | copy-done | bytes 1572888
  4.2 0.0 copy-start.2
  4.2 1.4 %copy-done.2 = bf16[1,768,1024]{2,1,0:T(8,128)(2,1)S(1)} copy-done((bf16[1,768,1024]{2,1,0:T(8,128)(2,1)S(1)}, bf16[1,768,1024]{2,1,0:T(8,128)(2,1)}, u32[]{:S(2)}) %copy-start.2) | copy-done | bytes 1572888
  5.6 0.0 copy-start.3
  5.6 0.9 copy-done.3
  6.5 0.0 copy-start.4
  6.5 0.9 copy-done.4
  7.5 95.8 %shard_map.102 = (bf16[128,1024]{1,0:T(8,128)(2,1)S(1)}, bf16[1,1024,768]{2,1,0:T(8,128)(2,1)S(1)}, bf16[1,1024,768]{2,1,0:T(8,128)(2,1)S(1)}, bf16[1,768,1024]{2,1,0:T(8,128)(2,1)S(1)}) custom-call(bf16[128,1024]{1,0:T(8,128)(2,1)S(1)} %copy-done.3, bf16[128,1024]{1,0:T(8,128)(2,1)S(1)} %copy-done.4, f32[8,128]{1,0:T(8,128)S(1)} %select_reduce_fusion.pe_ref, ...), custom_call_target="tpu_custom_call" | custom-call | tf_op jit(solution)/shard_map/pallas_call | solution.py:438
  103.2 0.7 copy.17
  104.0 1.1 %copy.18 = bf16[1,1024,768]{2,1,0:T(8,128)(2,1)} copy(bf16[1,1024,768]{2,1,0:T(8,128)(2,1)S(1)} %get-tuple-element.9) | data formatting | bytes 3145728
  105.1 1.1 %copy.19 = bf16[1,1024,768]{2,1,0:T(8,128)(2,1)} copy(bf16[1,1024,768]{2,1,0:T(8,128)(2,1)S(1)} %get-tuple-element.10) | data formatting | bytes 3145728
  106.2 1.1 %copy.20 = bf16[1,768,1024]{2,1,0:T(8,128)(2,1)} copy(bf16[1,768,1024]{2,1,0:T(8,128)(2,1)S(1)} %get-tuple-element.11) | data formatting | bytes 3145728
Async XLA Ops:
  1.3 1.4 %copy-start = (bf16[1,1024,768]{2,1,0:T(8,128)(2,1)S(1)}, bf16[1,1024,768]{2,1,0:T(8,128)(2,1)}, u32[]{:S(2)}) copy-start(bf16[1,1024,768]{2,1,0:T(8,128)(2,1)} %wg_hbm.1) | copy-start | bytes 4718596
  2.7 1.4 %copy-start.1 = (bf16[1,1024,768]{2,1,0:T(8,128)(2,1)S(1)}, bf16[1,1024,768]{2,1,0:T(8,128)(2,1)}, u32[]{:S(2)}) copy-start(bf16[1,1024,768]{2,1,0:T(8,128)(2,1)} %wu_hbm.1) | copy-start | bytes 4718596
  4.2 1.4 %copy-start.2 = (bf16[1,768,1024]{2,1,0:T(8,128)(2,1)S(1)}, bf16[1,768,1024]{2,1,0:T(8,128)(2,1)}, u32[]{:S(2)}) copy-start(bf16[1,768,1024]{2,1,0:T(8,128)(2,1)} %wd_hbm.1) | copy-start | bytes 4718596
  5.6 0.9 copy-start.3
  6.5 0.9 copy-start.4

commit v4 on v3

--- a/solution.py
+++ b/solution.py
@@ -275,7 +275,22 @@
     a_copies = [None] * chunks
     d_copies = [None] * n_ep
 
+    def send_partials(c, first, count):
+        for j, other in enumerate((near, flipped(q, 3))):
+            r, l = piece(other)
+            n = len(p_copies[c])
+            copy = remote(
+                pb.at[c, pl.ds(first, count), r, l],
+                rb.at[c, j, pl.ds(first, count)],
+                ps_sem.at[c, n],
+                pr_sem.at[c, n],
+                (e, near),
+            )
+            copy.start()
+            p_copies[c].append(copy)
+
     def partials(c):
+        p_copies[c] = []
         span = pl.ds(c * pair, pair)
         x_copies[c][0].wait_recv()
         if c == 0:
@@ -284,32 +299,28 @@
         x = rx[0, span, :]
         pb[c, 0] = jnp.dot(x, wg[...], preferred_element_type=F32).astype(BF16)
         pb[c, 1] = jnp.dot(x, wu[...], preferred_element_type=F32).astype(BF16)
+        send_partials(c, 0, 2)
         x_copies[c][1].wait_recv()
         pb[c, 2] = contract_cols(rx[1, span, :], wd[...]).astype(BF16)
-        p_copies[c] = []
-        for j, other in enumerate((near, flipped(q, 3))):
-            r, l = piece(other)
+        send_partials(c, 2, 1)
+
+    def pair_sum(c):
+        r, l = piece(far)
+        q_copies[c] = []
+        for n, (first, count) in enumerate(((0, 2), (2, 1))):
+            p_copies[c][2 * n + 1].wait_recv()
+            for i in range(first, first + count):
+                sb[c, i] = (pb[c, i, r, l].astype(F32) + rb[c, 1, i].astype(F32)).astype(BF16)
+            span = pl.ds(first, count)
             copy = remote(
-                pb.at[c, :, r, l],
-                rb.at[c, j],
-                ps_sem.at[c, j],
-                pr_sem.at[c, j],
-                (e, near),
+                sb.at[c, span], rb2.at[c, span], qs_sem.at[c, n], qr_sem.at[c, n], (e, far)
             )
             copy.start()
-            p_copies[c].append(copy)
-
-    def pair_sum(c):
-        p_copies[c][1].wait_recv()
-        r, l = piece(far)
-        for i in range(3):
-            sb[c, i] = (pb[c, i, r, l].astype(F32) + rb[c, 1, i].astype(F32)).astype(BF16)
-        q_copies[c] = remote(sb.at[c], rb2.at[c], qs_sem.at[c], qr_sem.at[c], (e, far))
-        q_copies[c].start()
+            q_copies[c].append(copy)
 
     def activate(c):
-        p_copies[c][0].wait_recv()
-        q_copies[c].wait_recv()
+        for copy in p_copies[c][0::2] + q_copies[c]:
+            copy.wait_recv()
         r, l = piece(q)
         gate, up, dact = [
             pb[c, i, r, l].astype(F32) + rb[c, 0, i].astype(F32) + rb2[c, i].astype(F32)
@@ -419,7 +430,7 @@
                 for i in range(2):
                     hop(direction, distance, i).wait_send()
 
-    for copy in pe_copies[1:] + q_copies + d_copies[1:] + sum(x_copies + p_copies + a_copies, []):
+    for copy in pe_copies[1:] + d_copies[1:] + sum(x_copies + p_copies + q_copies + a_copies, []):
         copy.wait_send()
     for copy in stores:
         copy.wait()
@@ -475,10 +486,10 @@
             dma((2, chunks, 2)),
             dma((chunks, 2)),
             dma((chunks, 2)),
+            dma((chunks, 4)),
+            dma((chunks, 4)),
             dma((chunks, 2)),
             dma((chunks, 2)),
-            dma((chunks,)),
-            dma((chunks,)),
             dma((chunks, 3)),
             dma((chunks, 3)),
             dma((n_ep,)),

time: 108 us -> 103 us (0.954)
  Pallas kernels: 95.8 us -> 90.8 us
    pallas_call x1, Pallas kernels: 95.8 us -> 90.8 us  [fused_on_device(): pl.pallas_call(functools.partial(fused_kernel, n_ep, n_tp, rows), out_sha...]
where the time goes in v4:
time: 103 us; the launch traced here: 102 us
  Pallas kernels  90.8 us (88%)
  local copies, waits for them, and re-layouts  10.3 us (10%)
    pallas_call x1, Pallas kernels, fused_on_device(): pl.pallas_call(functools.partial(fused_kernel, n_ep, n_tp, rows), out_sha...  90.8 us
    unnamed x14, local copies, waits for them, and re-layouts  10.3 us

profile of v4, /device:TPU:9, one launch (start us, length us, event | category | flops | bytes accessed | tf_op | source)
XLA Modules:
  0.0 102.4 jit_solution(11186232382168565661)
XLA Ops:
  0.6 0.7 select_reduce_fusion.pe_ref
  1.3 0.0 copy-start
  1.3 1.4 %copy-done = bf16[1,1024,768]{2,1,0:T(8,128)(2,1)S(1)} copy-done((bf16[1,1024,768]{2,1,0:T(8,128)(2,1)S(1)}, bf16[1,1024,768]{2,1,0:T(8,128)(2,1)}, u32[]{:S(2)}) %copy-start) | copy-done | bytes 1572888
  2.7 0.0 copy-start.1
  2.8 1.4 %copy-done.1 = bf16[1,1024,768]{2,1,0:T(8,128)(2,1)S(1)} copy-done((bf16[1,1024,768]{2,1,0:T(8,128)(2,1)S(1)}, bf16[1,1024,768]{2,1,0:T(8,128)(2,1)}, u32[]{:S(2)}) %copy-start.1) | copy-done | bytes 1572888
  4.2 0.0 copy-start.2
  4.2 1.4 %copy-done.2 = bf16[1,768,1024]{2,1,0:T(8,128)(2,1)S(1)} copy-done((bf16[1,768,1024]{2,1,0:T(8,128)(2,1)S(1)}, bf16[1,768,1024]{2,1,0:T(8,128)(2,1)}, u32[]{:S(2)}) %copy-start.2) | copy-done | bytes 1572888
  5.6 0.0 copy-start.3
  5.6 0.9 copy-done.3
  6.5 0.0 copy-start.4
  6.5 0.9 copy-done.4
  7.5 90.8 %shard_map.102 = (bf16[128,1024]{1,0:T(8,128)(2,1)S(1)}, bf16[1,1024,768]{2,1,0:T(8,128)(2,1)S(1)}, bf16[1,1024,768]{2,1,0:T(8,128)(2,1)S(1)}, bf16[1,768,1024]{2,1,0:T(8,128)(2,1)S(1)}) custom-call(bf16[128,1024]{1,0:T(8,128)(2,1)S(1)} %copy-done.3, bf16[128,1024]{1,0:T(8,128)(2,1)S(1)} %copy-done.4, f32[8,128]{1,0:T(8,128)S(1)} %select_reduce_fusion.pe_ref, ...), custom_call_target="tpu_custom_call" | custom-call | tf_op jit(solution)/shard_map/pallas_call | solution.py:449
  98.2 0.7 copy.17
  98.9 1.1 %copy.18 = bf16[1,1024,768]{2,1,0:T(8,128)(2,1)} copy(bf16[1,1024,768]{2,1,0:T(8,128)(2,1)S(1)} %get-tuple-element.9) | data formatting | bytes 3145728
  100.1 1.1 %copy.19 = bf16[1,1024,768]{2,1,0:T(8,128)(2,1)} copy(bf16[1,1024,768]{2,1,0:T(8,128)(2,1)S(1)} %get-tuple-element.10) | data formatting | bytes 3145728
  101.2 1.1 %copy.20 = bf16[1,768,1024]{2,1,0:T(8,128)(2,1)} copy(bf16[1,768,1024]{2,1,0:T(8,128)(2,1)S(1)} %get-tuple-element.11) | data formatting | bytes 3145728
Async XLA Ops:
  1.3 1.4 %copy-start = (bf16[1,1024,768]{2,1,0:T(8,128)(2,1)S(1)}, bf16[1,1024,768]{2,1,0:T(8,128)(2,1)}, u32[]{:S(2)}) copy-start(bf16[1,1024,768]{2,1,0:T(8,128)(2,1)} %wg_hbm.1) | copy-start | bytes 4718596
  2.7 1.4 %copy-start.1 = (bf16[1,1024,768]{2,1,0:T(8,128)(2,1)S(1)}, bf16[1,1024,768]{2,1,0:T(8,128)(2,1)}, u32[]{:S(2)}) copy-start(bf16[1,1024,768]{2,1,0:T(8,128)(2,1)} %wu_hbm.1) | copy-start | bytes 4718596
  4.2 1.4 %copy-start.2 = (bf16[1,768,1024]{2,1,0:T(8,128)(2,1)S(1)}, bf16[1,768,1024]{2,1,0:T(8,128)(2,1)}, u32[]{:S(2)}) copy-start(bf16[1,768,1024]{2,1,0:T(8,128)(2,1)} %wd_hbm.1) | copy-start | bytes 4718596
  5.6 0.9 copy-start.3
  6.5 0.9 copy-start.4
